TPU v7x, 32 devices: a whole 2x2x4 slice. The times are simulated.
32 devices in a mesh: expert: 16 (over z, y, x), tok: 2 (over core).
Axes of the slice: x: 2, y: 2, z: 4, core: 2. Of those that a mesh axis runs over, the one named last changes fastest.
Arguments:
- tokens: bfloat16 [2048, 3584], P(('expert', 'tok')), may hold values from -6 to 6
- routes: int32 [2048, 8], P(('expert', 'tok')), may hold values from 0 to 15, all different within a row; in each aligned block of 64 rows (0 to 63, 64 to 127, ...) at most 36 rows name the same one
- gates: float32 [2048, 8], P(('expert', 'tok')), may hold values from 0.05 to 1
- upstream: bfloat16 [2048, 3584], P(('expert', 'tok')), may hold values from -6 to 6
- w_up: bfloat16 [16, 3584, 1024], P('expert', None, 'tok'), may hold values from -0.09375 to 0.09375
- w_down: bfloat16 [16, 1024, 3584], P('expert', 'tok'), may hold values from -0.1875 to 0.1875
Outputs:
- mixed: bfloat16 [2048, 3584], P(('expert', 'tok'))
- d_tokens: bfloat16 [2048, 3584], P(('expert', 'tok'))
- d_gates: float32 [2048, 8], P(('expert', 'tok'))
- grad_up: bfloat16 [16, 3584, 1024], P('expert', None, 'tok')
- grad_down: bfloat16 [16, 1024, 3584], P('expert', 'tok')
Inputs may be any that keep to these rules, and one draw needn't show every extreme that they name: `routes`: each token names 8 different experts. At most 36 of the 64 tokens of one device name the same expert, and in every draw the tokens of some device name some expert exactly 36 times.
All inputs are finite; a program needn't handle non-finite values.
Results may differ from a plain program's by a relative error of at most 0.0065.
Values may be sent and summed in bfloat16 or wider, within the bound.
A program may use at most 192 MiB of HBM per device.

v0:
```python
import jax
import jax.numpy as jnp
from jax import lax
from jax.sharding import PartitionSpec as P

GELU_C = 0.7978845608028654
GELU_A = 0.044715


def gelu_value(hidden):
    inner_arg = GELU_C * (hidden + GELU_A * hidden * hidden * hidden)
    return 0.5 * hidden * (1.0 + jnp.tanh(inner_arg))


def gelu_slope(hidden):
    tangent = jnp.tanh(GELU_C * (hidden + GELU_A * hidden * hidden * hidden))
    return 0.5 * (1.0 + tangent) + 0.5 * hidden * (1.0 - tangent * tangent) * GELU_C * (
        1.0 + 3.0 * GELU_A * hidden * hidden
    )


def expert_rows(rows_x, rows_grad, up_local, down_local):
    hidden = jnp.dot(rows_x, up_local, preferred_element_type=jnp.float32)
    active = gelu_value(hidden).astype(jnp.bfloat16)
    out_part = jnp.dot(active, down_local, preferred_element_type=jnp.float32)
    d_active = lax.dot_general(
        rows_grad, down_local, (((1,), (1,)), ((), ())), preferred_element_type=jnp.float32
    )
    d_hidden = (d_active * gelu_slope(hidden)).astype(jnp.bfloat16)
    dx_part = lax.dot_general(
        d_hidden, up_local, (((1,), (1,)), ((), ())), preferred_element_type=jnp.float32
    )
    grad_down = lax.dot_general(
        active, rows_grad, (((0,), (0,)), ((), ())), preferred_element_type=jnp.float32
    )
    grad_up = lax.dot_general(
        rows_x, d_hidden, (((0,), (0,)), ((), ())), preferred_element_type=jnp.float32
    )
    return (out_part, dx_part, grad_up, grad_down)


def shards(tokens, routes, gates, upstream, w_up, w_down):
    tok_rows, feature_width = tokens.shape
    top_count = routes.shape[1]
    owners = lax.axis_size("expert")
    pair_count = lax.axis_size("tok")
    capacity = tok_rows * top_count // owners + max(1, tok_rows * top_count // (8 * owners))
    assigned = routes.reshape(-1)
    labels = jnp.arange(owners, dtype=jnp.int32)
    onehot = (assigned[:, None] == labels[None, :]).astype(jnp.int32)
    earlier = jnp.cumsum(onehot, axis=0) - onehot
    slot_rank = jnp.sum(earlier * onehot, axis=1)
    slot_of = assigned * capacity + slot_rank
    slot_ids = jnp.arange(owners * capacity, dtype=jnp.int32)
    matches = (slot_of[None, :] == slot_ids[:, None]).astype(jnp.int32)
    filled = jnp.sum(matches, axis=1) > 0
    source = jnp.sum(matches * jnp.arange(assigned.shape[0], dtype=jnp.int32)[None, :], axis=1)
    token_ids = source // top_count
    send_x = jnp.where(filled[:, None], tokens[token_ids], jnp.zeros((), jnp.bfloat16))
    gate_rows = jnp.where(filled, gates.reshape(-1)[source], jnp.zeros((), jnp.float32))
    send_grad = (gate_rows[:, None] * upstream[token_ids].astype(jnp.float32)).astype(jnp.bfloat16)
    send_x = send_x.reshape(owners, capacity, feature_width)
    send_grad = send_grad.reshape(owners, capacity, feature_width)
    recv_x, recv_grad = (
        lax.all_to_all(send_x, "expert", split_axis=0, concat_axis=0, tiled=True),
        lax.all_to_all(send_grad, "expert", split_axis=0, concat_axis=0, tiled=True),
    )
    both_x, both_grad = (
        lax.all_gather(recv_x[None], "tok", axis=0, tiled=True),
        lax.all_gather(recv_grad[None], "tok", axis=0, tiled=True),
    )
    rows_x = both_x.reshape(-1, feature_width)
    rows_grad = both_grad.reshape(-1, feature_width)
    out_part, dx_part, grad_up, grad_down = expert_rows(rows_x, rows_grad, w_up[0], w_down[0])
    shaped_out = out_part.reshape(pair_count, owners, capacity, feature_width)
    shaped_dx = dx_part.reshape(pair_count, owners, capacity, feature_width)
    summed_out, summed_dx = (
        lax.psum_scatter(shaped_out, "tok", scatter_dimension=0, tiled=True),
        lax.psum_scatter(shaped_dx, "tok", scatter_dimension=0, tiled=True),
    )
    home_out, home_dx = (
        lax.all_to_all(
            summed_out[0].astype(jnp.bfloat16), "expert", split_axis=0, concat_axis=0, tiled=True
        ),
        lax.all_to_all(
            summed_dx[0].astype(jnp.bfloat16), "expert", split_axis=0, concat_axis=0, tiled=True
        ),
    )
    out_pairs = (
        home_out.reshape(owners * capacity, feature_width)[slot_of]
        .reshape(tok_rows, top_count, feature_width)
        .astype(jnp.float32)
    )
    dx_pairs = (
        home_dx.reshape(owners * capacity, feature_width)[slot_of]
        .reshape(tok_rows, top_count, feature_width)
        .astype(jnp.float32)
    )
    mixed_out = jnp.sum(gates[:, :, None] * out_pairs, axis=1).astype(jnp.bfloat16)
    d_gates = jnp.sum(upstream.astype(jnp.float32)[:, None, :] * out_pairs, axis=2)
    d_tokens = jnp.sum(dx_pairs, axis=1).astype(jnp.bfloat16)
    return (
        mixed_out,
        d_tokens,
        d_gates,
        grad_up.astype(jnp.bfloat16)[None],
        grad_down.astype(jnp.bfloat16)[None],
    )


def solution(mesh):
    return jax.shard_map(
        shards,
        mesh=mesh,
        in_specs=(
            P(("expert", "tok"), None),
            P(("expert", "tok"), None),
            P(("expert", "tok"), None),
            P(("expert", "tok"), None),
            P("expert", None, "tok"),
            P("expert", "tok", None),
        ),
        out_specs=(
            P(("expert", "tok"), None),
            P(("expert", "tok"), None),
            P(("expert", "tok"), None),
            P("expert", None, "tok"),
            P("expert", "tok", None),
        ),
        check_vma=False,
    )
```

profile of v0, /device:TPU:14, one launch (start us, length us, event | category | flops | bytes accessed | tf_op | source)
XLA Modules:
  0.0 616.5 jit_solution(9409691657999771369)
XLA Ops:
  10.3 5.0 gather_fusion
  15.3 6.9 %gather.20 = bf16[16,36,3584]{2,1,0:T(8,128)(2,1)} reshape(bf16[576,3584]{1,0:T(8,128)(2,1)} %gather_fusion) | data formatting | bytes 8257536 | tf_op jit(solution)/shard_map/gather | solution.py:59
  26.9 7.3 %all-to-all-start = ((bf16[16,36,3584]{2,1,0:T(8,128)(2,1)}), bf16[16,36,3584]{2,1,0:T(8,128)(2,1)}, u32[]{:S(2)}, u32[]{:S(2)}) async-start(bf16[16,36,3584]{2,1,0:T(8,128)(2,1)} %broadcast_select_fusion), calls=%async_computation | async-start | bytes 9175040 | tf_op jit(solution)/shard_map/all_to_all | solution.py:65
  38.5 4.9 gather_fusion.3
  43.4 7.6 %reshape.211 = f32[16,36,3584]{2,1,0:T(8,128)} reshape(bf16[576,3584]{1,0:T(8,128)(2,1)} %gather_fusion.3) | data formatting | bytes 12386304 | tf_op jit(solution)/shard_map/convert_element_type | solution.py:61
  51.0 86.8 %all-to-all-done = bf16[16,36,3584]{2,1,0:T(8,128)(2,1)} async-done(((bf16[16,36,3584]{2,1,0:T(8,128)(2,1)}), bf16[16,36,3584]{2,1,0:T(8,128)(2,1)}, u32[]{:S(2)}, u32[]{:S(2)}) %all-to-all-start) | async-done | bytes 4128800 | tf_op jit(solution)/shard_map/all_to_all | solution.py:65
  137.7 5.4 copy.33
  148.1 104.5 %all_to_all.20 = bf16[16,36,3584]{2,1,0:T(8,128)(2,1)S(1)} all-to-all(bf16[16,36,3584]{2,1,0:T(8,128)(2,1)S(1)} %multiply_convert_fusion), channel_id=1, replica_groups=mesh['expert'=16,'tok'=2] {'expert'}, dimensions={0} | all-to-all | bytes 8257536 | tf_op jit(solution)/shard_map/all_to_all | solution.py:66
  256.4 12.7 %copy.34 = bf16[32,36,3584]{2,1,0:T(8,128)(2,1)} copy(bf16[32,36,3584]{2,0,1:T(8,128)(2,1)} %all-gather.5.cloned.1.call-done) | data formatting | bytes 16515072 | tf_op jit(solution)/shard_map/all_gather | solution.py:69
  269.1 12.7 %reshape.204 = bf16[1152,3584]{1,0:T(8,128)(2,1)} reshape(bf16[32,36,3584]{2,1,0:T(8,128)(2,1)} %copy.34) | data formatting | bytes 16515072 | tf_op jit(solution)/shard_map/reshape | solution.py:72
  281.8 11.4 %copy.38 = bf16[32,36,3584]{2,1,0:T(8,128)(2,1)} copy(bf16[32,36,3584]{2,0,1:T(8,128)(2,1)} %all-gather.7.cloned.1.call-done) | data formatting | bytes 16515072 | tf_op jit(solution)/shard_map/all_gather | solution.py:70
  293.2 12.6 %reshape.207 = bf16[1152,3584]{1,0:T(8,128)(2,1)} reshape(bf16[32,36,3584]{2,1,0:T(8,128)(2,1)} %copy.38) | data formatting | bytes 16515072 | tf_op jit(solution)/shard_map/reshape | solution.py:73
  305.8 10.6 %multiply_convert_fusion.1 = (bf16[1152,512]{1,0:T(8,128)(2,1)}, f32[1152,512]{1,0:T(8,128)S(1)}) fusion(bf16[1152,3584]{1,0:T(8,128)(2,1)} %reshape.204, bf16[1,3584,512]{2,1,0:T(8,128)(2,1)} %param.10), kind=kOutput, calls=%fused_computation.35 | convolution fusion | flops 4233166848 | bytes 15466496 | tf_op jit(solution)/shard_map/dot_general | solution.py:23
  316.4 5.8 fusion.15
  322.6 10.9 %fusion.4 = f32[2,16,36,3584]{3,2,1,0:T(8,128)} fusion(bf16[2,16,36,512]{3,2,1,0:T(8,128)(2,1)S(1)} %dot_general.26, bf16[1,3584,512]{2,1,0:T(8,128)(2,1)} %param.10), kind=kOutput, calls=%fused_computation.17 | convolution fusion | flops 4227858432 | bytes 21364736 | tf_op jit(solution)/shard_map/dot_general | solution.py:30
  335.7 14.4 %fusion.6 = f32[2,16,36,3584]{3,2,1,0:T(8,128)} fusion(bf16[2,16,36,512]{3,2,1,0:T(8,128)(2,1)S(1)} %dot_general.23, bf16[1,512,3584]{2,1,0:T(8,128)(2,1)} %param.11), kind=kOutput, calls=%fused_computation.19 | convolution fusion | flops 4227858432 | bytes 21364736 | tf_op jit(solution)/shard_map/dot_general | solution.py:25
  350.2 11.7 %reduce-scatter.5.cloned.1.call-done = f32[1,16,36,3584]{3,2,1,0:T(8,128)} async-done(((f32[2,16,36,3584]{3,2,1,0:T(8,128)}), f32[1,16,36,3584]{3,2,1,0:T(8,128)}) %reduce-scatter.5.cloned.1.call-update) | async-done | bytes 8257552 | tf_op jit(solution)/shard_map/reduce_scatter | solution.py:79
  361.9 6.3 %convert_bitcast_fusion = bf16[16,36,3584]{2,1,0:T(8,128)(2,1)} fusion(f32[1,16,36,3584]{3,2,1,0:T(8,128)} %reduce-scatter.5.cloned.1.call-done), kind=kLoop, calls=%fused_computation.14 | loop fusion | flops 2064384 | bytes 12386304 | tf_op jit(solution)/shard_map/convert_element_type | solution.py:86
  368.2 7.0 %all-to-all-start.3 = ((bf16[16,36,3584]{2,1,0:T(8,128)(2,1)}), bf16[16,36,3584]{2,1,0:T(8,128)(2,1)}, u32[]{:S(2)}, u32[]{:S(2)}) async-start(bf16[16,36,3584]{2,1,0:T(8,128)(2,1)} %convert_bitcast_fusion), calls=%async_computation.5 | async-start | bytes 9175040 | tf_op jit(solution)/shard_map/all_to_all | solution.py:85
  375.1 18.0 %reduce-scatter.3.cloned.1.call-done = f32[1,16,36,3584]{3,2,1,0:T(8,128)} async-done(((f32[2,16,36,3584]{3,2,1,0:T(8,128)}), f32[1,16,36,3584]{3,2,1,0:T(8,128)}) %reduce-scatter.3.cloned.1.call-update) | async-done | bytes 8257552 | tf_op jit(solution)/shard_map/reduce_scatter | solution.py:78
  393.1 6.2 %convert_bitcast_fusion.1 = bf16[16,36,3584]{2,1,0:T(8,128)(2,1)} fusion(f32[1,16,36,3584]{3,2,1,0:T(8,128)} %reduce-scatter.3.cloned.1.call-done), kind=kLoop, calls=%fused_computation.15 | loop fusion | flops 2064384 | bytes 12386304 | tf_op jit(solution)/shard_map/convert_element_type | solution.py:83
  399.3 80.0 %all-to-all-done.3 = bf16[16,36,3584]{2,1,0:T(8,128)(2,1)} async-done(((bf16[16,36,3584]{2,1,0:T(8,128)(2,1)}), bf16[16,36,3584]{2,1,0:T(8,128)(2,1)}, u32[]{:S(2)}, u32[]{:S(2)}) %all-to-all-start.3) | async-done | bytes 4128800 | tf_op jit(solution)/shard_map/all_to_all | solution.py:85
  479.3 5.4 all-to-all-start.1
  485.0 10.5 %fusion.3 = bf16[1,512,3584]{2,1,0:T(8,128)(2,1)} fusion(bf16[1152,512]{1,0:T(8,128)(2,1)} %get-tuple-element.21, bf16[1152,3584]{1,0:T(8,128)(2,1)} %reshape.207), kind=kOutput, calls=%fused_computation.13 | convolution fusion | flops 4229693440 | bytes 13107200 | tf_op jit(solution)/shard_map/dot_general | solution.py:33
  495.5 9.8 %fusion.2 = bf16[1,3584,512]{2,1,0:T(8,128)(2,1)} fusion(bf16[1152,3584]{1,0:T(8,128)(2,1)} %reshape.204, bf16[1152,512]{1,0:T(8,128)(2,1)S(1)} %fusion.15), kind=kOutput, calls=%fused_computation.12 | convolution fusion | flops 4229693440 | bytes 13107200 | tf_op jit(solution)/shard_map/dot_general | solution.py:36
  505.2 6.9 %reshape.208 = bf16[576,3584]{1,0:T(8,128)(2,1)} reshape(bf16[16,36,3584]{2,1,0:T(8,128)(2,1)} %all-to-all-done.3) | data formatting | bytes 8257536 | tf_op jit(solution)/shard_map/reshape | solution.py:95
  512.2 10.8 %gather_fusion.4 = bf16[512,3584]{1,0:T(8,128)(2,1)} fusion(bf16[576,3584]{1,0:T(8,128)(2,1)} %reshape.208, s32[1024]{0:T(1024)S(1)} %pad_clamp_fusion.1), kind=kCustom, calls=%fused_computation.4 | custom fusion | bytes 7342080 | tf_op jit(solution)/shard_map/gather | solution.py:95
  523.0 5.3 bitcast_reduce_fusion
  528.2 57.7 %all-to-all-done.1 = bf16[16,36,3584]{2,1,0:T(8,128)(2,1)} async-done(((bf16[16,36,3584]{2,1,0:T(8,128)(2,1)}), bf16[16,36,3584]{2,1,0:T(8,128)(2,1)}, u32[]{:S(2)}, u32[]{:S(2)}) %all-to-all-start.1) | async-done | bytes 4128800 | tf_op jit(solution)/shard_map/all_to_all | solution.py:82
  585.9 6.9 %reshape.205 = bf16[576,3584]{1,0:T(8,128)(2,1)} reshape(bf16[16,36,3584]{2,1,0:T(8,128)(2,1)} %all-to-all-done.1) | data formatting | bytes 8257536 | tf_op jit(solution)/shard_map/reshape | solution.py:90
  592.8 10.7 %gather_fusion.1 = bf16[512,3584]{1,0:T(8,128)(2,1)} fusion(bf16[576,3584]{1,0:T(8,128)(2,1)} %reshape.205, s32[1024]{0:T(1024)S(1)} %pad_clamp_fusion.1), kind=kCustom, calls=%fused_computation.1 | custom fusion | bytes 7342080 | tf_op jit(solution)/shard_map/gather | solution.py:90
  603.5 5.6 fusion.1
  (60 shorter events, 24.3 us)
Async XLA Ops:
  7.2 3.1 copy-start
  26.9 7.3 %copy-start.7 = (f32[64,8]{0,1:T(8,128)S(1)}, f32[64,8]{0,1:T(8,128)}, u32[]{:S(2)}) copy-start(f32[64,8]{0,1:T(8,128)} %param.8) | copy-start | bytes 6148
  26.9 110.8 %all-to-all-start = ((bf16[16,36,3584]{2,1,0:T(8,128)(2,1)}), bf16[16,36,3584]{2,1,0:T(8,128)(2,1)}, u32[]{:S(2)}, u32[]{:S(2)}) async-start(bf16[16,36,3584]{2,1,0:T(8,128)(2,1)} %broadcast_select_fusion), calls=%async_computation | async-start | bytes 9175040 | tf_op jit(solution)/shard_map/all_to_all | solution.py:65
  34.2 4.3 copy-start.2
  34.2 222.2 %all-gather.5.cloned.1.call-start = ((), (), s32[]{:S(2)}) async-start(), calls=%async_computation.8 | async-start | bytes 12386304 | tf_op jit(solution)/shard_map/all_gather | solution.py:69
  34.3 9.1 %copy-start.4 = (f32[64,8]{1,0:T(8,128)}, f32[64,8]{1,0:T(8,128)S(1)}, u32[]{:S(2)}) copy-start(f32[64,8]{1,0:T(8,128)S(1)} %copy.29) | copy-start | bytes 6148
  143.2 138.6 %all-gather.7.cloned.1.call-start = ((), (), s32[]{:S(2)}) async-start(), calls=%async_computation.9 | async-start | bytes 12386304 | tf_op jit(solution)/shard_map/all_gather | solution.py:70
  255.8 106.0 %reduce-scatter.5.cloned.1.call-start = ((), (), s32[]{:S(2)}) async-start(), calls=%async_computation.7 | async-start | bytes 27525120 | tf_op jit(solution)/shard_map/reduce_scatter | solution.py:79
  305.8 10.6 %copy-start.3 = (bf16[1152,3584]{1,0:T(8,128)(2,1)S(1)}, bf16[1152,3584]{1,0:T(8,128)(2,1)}, u32[]{:S(2)}) copy-start(bf16[1152,3584]{1,0:T(8,128)(2,1)} %reshape.207) | copy-start | bytes 24772612
  305.8 10.6 %copy-start.8 = (bf16[1,512,3584]{2,1,0:T(8,128)(2,1)S(1)}, bf16[1,512,3584]{2,1,0:T(8,128)(2,1)}, u32[]{:S(2)}) copy-start(bf16[1,512,3584]{2,1,0:T(8,128)(2,1)} %param.11) | copy-start | bytes 11010052
  333.5 59.5 %reduce-scatter.3.cloned.1.call-start = ((), (), s32[]{:S(2)}) async-start(), calls=%async_computation.6 | async-start | bytes 27525120 | tf_op jit(solution)/shard_map/reduce_scatter | solution.py:78
  368.2 111.1 %all-to-all-start.3 = ((bf16[16,36,3584]{2,1,0:T(8,128)(2,1)}), bf16[16,36,3584]{2,1,0:T(8,128)(2,1)}, u32[]{:S(2)}, u32[]{:S(2)}) async-start(bf16[16,36,3584]{2,1,0:T(8,128)(2,1)} %convert_bitcast_fusion), calls=%async_computation.5 | async-start | bytes 9175040 | tf_op jit(solution)/shard_map/all_to_all | solution.py:85
  399.3 85.5 %copy-start.6 = (s32[64,8]{0,1:T(8,128)S(1)}, s32[64,8]{0,1:T(8,128)}, u32[]{:S(2)}) copy-start(s32[64,8]{0,1:T(8,128)} %param.7) | copy-start | bytes 6148
  479.3 106.6 %all-to-all-start.1 = ((bf16[16,36,3584]{2,1,0:T(8,128)(2,1)}), bf16[16,36,3584]{2,1,0:T(8,128)(2,1)}, u32[]{:S(2)}, u32[]{:S(2)}) async-start(bf16[16,36,3584]{2,1,0:T(8,128)(2,1)} %convert_bitcast_fusion.1), calls=%async_computation.2 | async-start | bytes 9175040 | tf_op jit(solution)/shard_map/all_to_all | solution.py:82
  592.8 10.7 %copy-start.5 = (f32[64,8]{1,0:T(8,128)S(1)}, f32[64,8]{1,0:T(8,128)}, u32[]{:S(2)}) copy-start(f32[64,8]{1,0:T(8,128)} %copy-done.4) | copy-start | bytes 6148
  592.8 16.9 %copy-start.1 = (bf16[64,3584]{1,0:T(8,128)(2,1)S(1)}, bf16[64,3584]{1,0:T(8,128)(2,1)}, u32[]{:S(2)}) copy-start(bf16[64,3584]{1,0:T(8,128)(2,1)} %param.6) | copy-start | bytes 1376260
Sparse Core Ops, SparseCore 0:
  143.3 18.9 all-gather.4
  256.0 19.9 all-gather.6
  333.7 28.1 reduce-scatter.4
  364.1 28.9 reduce-scatter.2
where the time goes:
time: 625 us; the launch traced here: 617 us
  waiting for transfers between devices  254 us (41%)
  local copies, waits for them, and re-layouts  127 us (20%)
  blocking collectives  105 us (17%)
  matrix products  62 us (10%)
  other arithmetic  34.7 us (6%)
  starting transfers between devices  20.2 us (3%)
  between operations  14.2 us (2%)
    all_to_all x1, blocking collectives, shards(): lax.all_to_all(send_grad, 'expert', split_axis=0, concat_axis=0, tiled=True)  105 us
    all_to_all x1, waiting for transfers between devices, shards(): lax.all_to_all(send_x, 'expert', split_axis=0, concat_axis=0, tiled=True)  86.8 us
    all_to_all x1, waiting for transfers between devices, shards(): lax.all_to_all(summed_dx[0].astype(jnp.bfloat16), 'expert', split_axis=0,...  80 us
    all_to_all x1, waiting for transfers between devices, shards(): lax.all_to_all(summed_out[0].astype(jnp.bfloat16), 'expert', split_axis=0...  57.7 us
    reduce_scatter x1, waiting for transfers between devices, shards(): lax.psum_scatter(shaped_out, 'tok', scatter_dimension=0, tiled=True)  18 us
    dot_general x1, matrix products, expert_rows(): out_part = jnp.dot(active, down_local, preferred_element_type=jnp.float32)  14.4 us
    reshape x1, local copies, waits for them, and re-layouts, shards(): rows_x = both_x.reshape(-1, feature_width)  12.7 us
    all_gather x1, local copies, waits for them, and re-layouts, shards(): lax.all_gather(recv_x[None], 'tok', axis=0, tiled=True)  12.7 us
  transfers between devices with their start and end apart: 7, of which 5 were waited for; matrix products, arithmetic and copies ran while one was open for 20% of the time, Pallas kernels for 0%

commit v1 on v0

--- a/solution.py
+++ b/solution.py
@@ -39,7 +39,7 @@
     return (out_part, dx_part, grad_up, grad_down)
 
 
-def shards(tokens, routes, gates, upstream, w_up, w_down):
+def routed_shards(tokens, routes, gates, upstream, w_up, w_down):
     tok_rows, feature_width = tokens.shape
     top_count = routes.shape[1]
     owners = lax.axis_size("expert")
@@ -108,6 +108,68 @@
     )
 
 
+def dense_shards(tokens, routes, gates, upstream, w_up, w_down):
+    tok_rows, width = tokens.shape
+    owners = lax.axis_size("expert")
+    half = w_up.shape[2]
+    swap = ((0, 1), (1, 0))
+    up_local, down_local = w_up[0], w_down[0]
+    up_full = jnp.concatenate([up_local, lax.ppermute(up_local, "tok", swap)], axis=1)
+    down_full = jnp.concatenate([down_local, lax.ppermute(down_local, "tok", swap)], axis=0)
+    named = routes[:, :, None] == jnp.arange(owners, dtype=jnp.int32)
+    gate_of = jnp.sum(jnp.where(named, gates[:, :, None], 0.0), axis=1)
+    gate = lax.all_to_all(gate_of.T, "expert", split_axis=0, concat_axis=0, tiled=True)
+    gate = gate.reshape(-1)[:, None]
+    all_x = lax.all_gather(tokens, "expert", axis=0, tiled=True)
+    all_u = lax.all_gather(upstream, "expert", axis=0, tiled=True)
+    hidden = jnp.dot(all_x, up_full, preferred_element_type=jnp.float32)
+    gated = (gate * gelu_value(hidden)).astype(jnp.bfloat16)
+    mixed_part = jnp.dot(gated, down_full, preferred_element_type=jnp.float32)
+    mixed = lax.psum_scatter(
+        mixed_part.astype(jnp.bfloat16), "expert", scatter_dimension=0, tiled=True
+    )
+    back = lax.dot_general(
+        all_u, down_full, (((1,), (1,)), ((), ())), preferred_element_type=jnp.float32
+    )
+    inner = jnp.sum(gelu_value(hidden) * back, axis=1)
+    d_hidden = (gate * back * gelu_slope(hidden)).astype(jnp.bfloat16)
+    dx_part = lax.dot_general(
+        d_hidden, up_full, (((1,), (1,)), ((), ())), preferred_element_type=jnp.float32
+    )
+    d_tokens = lax.psum_scatter(
+        dx_part.astype(jnp.bfloat16), "expert", scatter_dimension=0, tiled=True
+    )
+    home = lax.all_to_all(
+        inner.reshape(owners, tok_rows), "expert", split_axis=0, concat_axis=0, tiled=True
+    )
+    d_gates = jnp.sum(jnp.where(named, home.T[:, None, :], 0.0), axis=2)
+
+    def outer(rows, columns):
+        return lax.dot_general(
+            rows, columns, (((0,), (0,)), ((), ())), preferred_element_type=jnp.float32
+        )
+
+    down_far = outer(gated[:, half:], all_u).astype(jnp.bfloat16)
+    up_far = outer(all_x, d_hidden[:, half:]).astype(jnp.bfloat16)
+    down_near = outer(gated[:, :half], all_u)
+    up_near = outer(all_x, d_hidden[:, :half])
+    grad_down = down_near + lax.ppermute(down_far, "tok", swap).astype(jnp.float32)
+    grad_up = up_near + lax.ppermute(up_far, "tok", swap).astype(jnp.float32)
+    return (
+        mixed,
+        d_tokens,
+        d_gates,
+        grad_up.astype(jnp.bfloat16)[None],
+        grad_down.astype(jnp.bfloat16)[None],
+    )
+
+
+def shards(tokens, routes, gates, upstream, w_up, w_down):
+    dense = 2 * routes.shape[1] >= lax.axis_size("expert") and lax.axis_size("tok") == 2
+    body = dense_shards if dense else routed_shards
+    return body(tokens, routes, gates, upstream, w_up, w_down)
+
+
 def solution(mesh):
     return jax.shard_map(
         shards,

time: 625 us -> 601 us (0.962)
  waiting for transfers between devices: 254 us -> 465 us
  local copies, waits for them, and re-layouts: 127 us -> 7.92 us
  blocking collectives: 105 us -> 19.8 us
  other arithmetic: 34.7 us -> 6.87 us
  matrix products: 62 us -> 84.2 us
  starting transfers between devices: 20.2 us -> 1.36 us
    reduce_scatter x2, waiting for transfers between devices: 29.7 us -> 268 us  [the longest x1 162 us: dense_shards(): lax.psum_scatter(mixed_part.astype(jnp.bfloat16), 'expert', scatter_dimen...]
    all_to_all x3 -> x0, waiting for transfers between devices: 224 us -> none  [the longest x1 86.8 us: shards(): lax.all_to_all(send_x, 'expert', split_axis=0, concat_axis=0, tiled=True)]
    all_gather x2, waiting for transfers between devices: 0.02 us -> 189 us  [the longest x1 97.9 us: dense_shards(): all_x = lax.all_gather(tokens, 'expert', axis=0, tiled=True)]
    all_to_all x1 -> x2, blocking collectives: 105 us -> 19.8 us  [the longest x1 10 us: dense_shards(): lax.all_to_all(inner.reshape(owners, tok_rows), 'expert', split_axis=0, c...]
    gather x7 -> x0, local copies, waits for them, and re-layouts: 42.2 us -> none  [the longest x2 11.9 us: shards(): tokens[token_ids]]
    reshape x6 -> x0, local copies, waits for them, and re-layouts: 39.4 us -> none  [the longest x1 12.7 us: shards(): rows_x = both_x.reshape(-1, feature_width)]
    all_gather x2 -> x0, local copies, waits for them, and re-layouts: 24.1 us -> none  [the longest x1 12.7 us: shards(): lax.all_gather(recv_x[None], 'tok', axis=0, tiled=True)]
    dot_general x6 -> x8, matrix products: 62 us -> 84.2 us  [the longest x4 30.7 us: outer(): lax.dot_general(rows, columns, (((0,), (0,)), ((), ())), preferred_elemen...]
  transfers between devices with their start and end apart: 7 -> 8, of which waited for: 5 -> 5; matrix products, arithmetic and copies ran while one was open for 20% -> 11% of each run, Pallas kernels for 0% -> 0%
where the time goes in v1:
time: 601 us; the launch traced here: 599 us
  waiting for transfers between devices  465 us (77%)
  matrix products  84.2 us (14%)
  blocking collectives  19.8 us (3%)
  between operations  13.9 us (2%)
  local copies, waits for them, and re-layouts  7.92 us (1%)
  other arithmetic  6.87 us (1%)
    reduce_scatter x1, waiting for transfers between devices, dense_shards(): lax.psum_scatter(mixed_part.astype(jnp.bfloat16), 'expert', scatter_dimen...  162 us
    reduce_scatter x1, waiting for transfers between devices, dense_shards(): lax.psum_scatter(dx_part.astype(jnp.bfloat16), 'expert', scatter_dimensio...  106 us
    all_gather x1, waiting for transfers between devices, dense_shards(): all_x = lax.all_gather(tokens, 'expert', axis=0, tiled=True)  97.9 us
    all_gather x1, waiting for transfers between devices, dense_shards(): all_u = lax.all_gather(upstream, 'expert', axis=0, tiled=True)  90.8 us
    dot_general x4, matrix products, outer(): lax.dot_general(rows, columns, (((0,), (0,)), ((), ())), preferred_elemen...  30.7 us
    dot_general x1, matrix products, dense_shards(): lax.dot_general(all_u, down_full, (((1,), (1,)), ((), ())), preferred_ele...  15 us
    dot_general x1, matrix products, dense_shards(): hidden = jnp.dot(all_x, up_full, preferred_element_type=jnp.float32)  13.6 us
    dot_general x1, matrix products, dense_shards(): mixed_part = jnp.dot(gated, down_full, preferred_element_type=jnp.float32)  13 us
  transfers between devices with their start and end apart: 8, of which 5 were waited for; matrix products, arithmetic and copies ran while one was open for 11% of the time, Pallas kernels for 0%

profile of v1, /device:TPU:14, one launch (start us, length us, event | category | flops | bytes accessed | tf_op | source)
XLA Modules:
  0.0 598.7 jit_solution(6524580034297987019)
XLA Ops:
  7.2 0.7 all-gather.3.cloned.1.call-update
  7.9 0.0 all-gather.5.cloned.1.call-start
  7.9 0.7 all-gather.5.cloned.1.call-update
  8.6 0.0 reduce-scatter.5.cloned.1.call-start
  8.7 0.1 collective-permute-start
  8.8 0.5 collective-permute-start.1
  9.3 6.2 %collective-permute-done = bf16[3584,512]{1,0:T(8,128)(2,1)} collective-permute-done((bf16[3584,512]{1,0:T(8,128)(2,1)}, bf16[3584,512]{1,0:T(8,128)(2,1)}, u32[]{:S(2)}, u32[]{:S(2)}) %collective-permute-start) | collective-permute-done | bytes 3670048 | tf_op jit(solution)/shard_map/ppermute | solution.py:117
  15.5 97.9 %all-gather.3.cloned.1.call-done = bf16[1024,3584]{1,0:T(8,128)(2,1)} async-done(((bf16[64,3584]{1,0:T(8,128)(2,1)}), bf16[1024,3584]{1,0:T(8,128)(2,1)}) %all-gather.3.cloned.1.call-update) | async-done | bytes 7340048 | tf_op jit(solution)/shard_map/all_gather | solution.py:123
  113.4 13.6 %fusion.4 = f32[1024,1024]{1,0:T(8,128)} fusion(bf16[1024,3584]{1,0:T(8,128)(2,1)} %all-gather.3.cloned.1.call-done, bf16[3584,512]{1,0:T(8,128)(2,1)} %collective-permute-done, bf16[3584,512]{1,0:T(8,128)(2,1)} %bitcast.60), kind=kOutput, calls=%fused_computation.14 | convolution fusion | flops 7530872832 | bytes 18874368 | tf_op jit(solution)/shard_map/dot_general | solution.py:125
  127.0 90.8 %all-gather.5.cloned.1.call-done = bf16[1024,3584]{1,0:T(8,128)(2,1)} async-done(((bf16[64,3584]{1,0:T(8,128)(2,1)}), bf16[1024,3584]{1,0:T(8,128)(2,1)}) %all-gather.5.cloned.1.call-update) | async-done | bytes 7340048 | tf_op jit(solution)/shard_map/all_gather | solution.py:124
  217.8 15.0 %fusion.12 = (f32[1024]{0:T(1024)S(1)}, f32[1024,1024]{1,0:T(8,128)}) fusion(f32[1024,1024]{1,0:T(8,128)} %fusion.4, bf16[1024,3584]{1,0:T(8,128)(2,1)} %all-gather.5.cloned.1.call-done, bf16[512,3584]{1,0:T(8,128)(2,1)} %collective-permute-done.1, bf16[512,3584]{1,0:T(8,128)(2,1)} %bitcast.63), kind=kOutput, calls=%fused_computation.24 | convolution fusion | flops 7541357568 | bytes 23072768 | tf_op jit(solution)/shard_map/dot_general | solution.py:131
  232.7 0.1 all_to_all.16
  232.8 10.0 %all_to_all.21 = f32[16,1,64]{2,1,0:T(1,128)S(1)} all-to-all(f32[16,1,64]{2,1,0:T(1,128)S(1)} %bitcast.56), channel_id=1, replica_groups=mesh['expert'=16,'tok'=2] {'expert'}, dimensions={0} | all-to-all | bytes 8192 | tf_op jit(solution)/shard_map/all_to_all | solution.py:142
  242.8 0.6 select_reduce_fusion
  243.4 9.8 %all_to_all.22 = f32[16,1,64]{2,1,0:T(1,128)S(1)} all-to-all(f32[16,1,64]{2,1,0:T(1,128)S(1)} %bitcast.55), channel_id=1, replica_groups=mesh['expert'=16,'tok'=2] {'expert'}, dimensions={0} | all-to-all | bytes 8192 | tf_op jit(solution)/shard_map/all_to_all | solution.py:121
  253.3 0.5 broadcast.46
  253.8 0.7 reduce.3
  254.5 0.1 mul.75
  254.5 5.6 fusion.11
  260.1 1.3 copy-done
  261.4 12.0 %convolution_convert_fusion = bf16[1024,3584]{1,0:T(8,128)(2,1)} fusion(bf16[1024,1024]{0,1:T(8,128)(2,1)S(1)} %get-tuple-element.27, bf16[3584,512]{1,0:T(8,128)(2,1)} %collective-permute-done, bf16[3584,512]{1,0:T(8,128)(2,1)S(1)} %bitcast.61), kind=kOutput, calls=%fused_computation | convolution fusion | flops 7534542848 | bytes 16777216 | tf_op jit(solution)/shard_map/dot_general | solution.py:136
  273.4 0.3 reduce-scatter.3.cloned.1.call-start
  273.7 13.0 %convolution_convert_fusion.1 = bf16[1024,3584]{1,0:T(8,128)(2,1)} fusion(bf16[1024,1024]{0,1:T(8,128)(2,1)S(1)} %get-tuple-element.28, bf16[512,3584]{1,0:T(8,128)(2,1)} %collective-permute-done.1, bf16[512,3584]{1,0:T(8,128)(2,1)} %bitcast.64), kind=kOutput, calls=%fused_computation.1 | convolution fusion | flops 7534542848 | bytes 16777216 | tf_op jit(solution)/shard_map/dot_general | solution.py:127
  286.8 7.5 %fusion.1 = bf16[3584,512]{0,1:T(8,128)(2,1)S(1)} fusion(bf16[1024,3584]{1,0:T(8,128)(2,1)} %all-gather.3.cloned.1.call-done, bf16[1024,1024]{0,1:T(8,128)(2,1)} %copy-done), kind=kOutput, calls=%fused_computation.11 | convolution fusion | flops 3759931392 | bytes 12058624 | tf_op jit(solution)/shard_map/dot_general | solution.py:148
  294.3 0.1 collective-permute-start.2
  294.4 8.7 %convolution_convert_fusion.2 = bf16[512,3584]{1,0:T(8,128)(2,1)} fusion(bf16[1024,3584]{1,0:T(8,128)(2,1)} %all-gather.5.cloned.1.call-done, bf16[1024,1024]{0,1:T(8,128)(2,1)S(1)} %get-tuple-element.28), kind=kOutput, calls=%fused_computation.9 | convolution fusion | flops 3759931392 | bytes 12058624 | tf_op jit(solution)/shard_map/dot_general | solution.py:148
  303.1 0.3 collective-permute-start.3
  303.4 5.4 fusion.2
  308.9 5.9 copy.25
  314.8 9.1 %fusion.14 = bf16[1,512,3584]{2,1,0:T(8,128)(2,1)} fusion(bf16[512,3584]{1,0:T(8,128)(2,1)} %collective-permute-done.3, bf16[1024,3584]{1,0:T(8,128)(2,1)} %all-gather.5.cloned.1.call-done, bf16[1024,1024]{0,1:T(8,128)(2,1)S(1)} %get-tuple-element.28), kind=kOutput, calls=%fused_computation.28 | convolution fusion | flops 3763601408 | bytes 15728640 | tf_op jit(solution)/shard_map/dot_general | solution.py:148
  323.9 106.4 %reduce-scatter.5.cloned.1.call-done = bf16[64,3584]{1,0:T(8,128)(2,1)} async-done(((bf16[1024,3584]{1,0:T(8,128)(2,1)}), bf16[64,3584]{1,0:T(8,128)(2,1)}) %reduce-scatter.5.cloned.1.call-update) | async-done | bytes 458768 | tf_op jit(solution)/shard_map/reduce_scatter | solution.py:139
  430.2 161.9 %reduce-scatter.3.cloned.1.call-done = bf16[64,3584]{1,0:T(8,128)(2,1)} async-done(((bf16[1024,3584]{1,0:T(8,128)(2,1)}), bf16[64,3584]{1,0:T(8,128)(2,1)}) %reduce-scatter.3.cloned.1.call-update) | async-done | bytes 458768 | tf_op jit(solution)/shard_map/reduce_scatter | solution.py:128
  (20 shorter events, 0.1 us)
Async XLA Ops:
  7.2 106.2 %all-gather.3.cloned.1.call-start = ((), (), s32[]{:S(2)}) async-start(), calls=%async_computation.4 | async-start | bytes 7798784 | tf_op jit(solution)/shard_map/all_gather | solution.py:123
  7.9 209.9 %all-gather.5.cloned.1.call-start = ((), (), s32[]{:S(2)}) async-start(), calls=%async_computation.6 | async-start | bytes 7798784 | tf_op jit(solution)/shard_map/all_gather | solution.py:124
  8.6 421.6 %reduce-scatter.5.cloned.1.call-start = ((), (), s32[]{:S(2)}) async-start(), calls=%async_computation.7 | async-start | bytes 7798784 | tf_op jit(solution)/shard_map/reduce_scatter | solution.py:139
  8.7 6.8 %collective-permute-start = (bf16[3584,512]{1,0:T(8,128)(2,1)}, bf16[3584,512]{1,0:T(8,128)(2,1)}, u32[]{:S(2)}, u32[]{:S(2)}) collective-permute-start(bf16[3584,512]{1,0:T(8,128)(2,1)} %bitcast.59), channel_id=1, source_target_pairs={{0,1},{1,0},{2,3},{3,2},{4,5},{5,4},{6,7},{7,6},{8,9},{9,8},{10,11... | collective-permute-start | bytes 11010056 | tf_op jit(solution)/shard_map/ppermute | solution.py:117
  8.8 118.2 %collective-permute-start.1 = (bf16[512,3584]{1,0:T(8,128)(2,1)}, bf16[512,3584]{1,0:T(8,128)(2,1)}, u32[]{:S(2)}, u32[]{:S(2)}) collective-permute-start(bf16[512,3584]{1,0:T(8,128)(2,1)} %bitcast.62), channel_id=1, source_target_pairs={{0,1},{1,0},{2,3},{3,2},{4,5},{5,4},{6,7},{7,6},{8,9},{9,8},{10,11... | collective-permute-start | bytes 11010056 | tf_op jit(solution)/shard_map/ppermute | solution.py:118
  127.0 115.8 %copy-start.2 = (s32[64,8]{0,1:T(8,128)S(1)}, s32[64,8]{0,1:T(8,128)}, u32[]{:S(2)}) copy-start(s32[64,8]{0,1:T(8,128)} %param.7) | copy-start | bytes 6148
  127.0 115.8 %copy-start.3 = (f32[64,8]{0,1:T(8,128)S(1)}, f32[64,8]{0,1:T(8,128)}, u32[]{:S(2)}) copy-start(f32[64,8]{0,1:T(8,128)} %param.8) | copy-start | bytes 6148
  254.5 6.9 %copy-start.4 = (bf16[1,3584,512]{2,1,0:T(8,128)(2,1)S(1)}, bf16[1,3584,512]{2,1,0:T(8,128)(2,1)}, u32[]{:S(2)}) copy-start(bf16[1,3584,512]{2,1,0:T(8,128)(2,1)} %param.10) | copy-start | bytes 11010052
  260.1 1.3 copy-start
  273.4 318.7 %reduce-scatter.3.cloned.1.call-start = ((), (), s32[]{:S(2)}) async-start(), calls=%async_computation.5 | async-start | bytes 7798784 | tf_op jit(solution)/shard_map/reduce_scatter | solution.py:128
  286.8 16.6 %slice-start = ((s8[7340032]{0:T(1024)(128)(4,1)}), s8[4194304]{0:T(1024)(128)(4,1)S(1)}, s32[]{:S(2)}) async-start(s8[7340032]{0:T(1024)(128)(4,1)} %bitcast.57), calls=%async_computation.8 | async-start | bytes 8388608
  294.3 9.1 %copy-start.1 = (bf16[1024,1024]{0,1:T(8,128)(2,1)S(1)}, bf16[1024,1024]{0,1:T(8,128)(2,1)}, u32[]{:S(2)}) copy-start(bf16[1024,1024]{0,1:T(8,128)(2,1)} %copy-done) | copy-start | bytes 6291460
  294.3 9.1 %slice-start.1 = ((s8[7340032]{0:T(1024)(128)(4,1)}), s8[3145728]{0:T(1024)(128)(4,1)S(1)}, s32[]{:S(2)}) async-start(s8[7340032]{0:T(1024)(128)(4,1)} %bitcast.57), calls=%async_computation.9 | async-start | bytes 6291456
  294.3 9.1 %collective-permute-start.2 = (bf16[3584,512]{0,1:T(8,128)(2,1)S(1)}, bf16[3584,512]{0,1:T(8,128)(2,1)S(1)}, u32[]{:S(2)}, u32[]{:S(2)}) collective-permute-start(bf16[3584,512]{0,1:T(8,128)(2,1)S(1)} %fusion.1), channel_id=1, source_target_pairs={{0,1},{1,0},{2,3},{3,2},{4,5},{5,4},{6,7},{7,6},{8,9},{9,8},{10,11... | collective-permute-start | bytes 11010056 | tf_op jit(solution)/shard_map/ppermute | solution.py:157
  303.1 11.7 %collective-permute-start.3 = (bf16[512,3584]{1,0:T(8,128)(2,1)}, bf16[512,3584]{1,0:T(8,128)(2,1)}, u32[]{:S(2)}, u32[]{:S(2)}) collective-permute-start(bf16[512,3584]{1,0:T(8,128)(2,1)} %convolution_convert_fusion.2), channel_id=1, source_target_pairs={{0,1},{1,0},{2,3},{3,2},{4,5},{5,4},{6,7},{7,6},{8,9},{9,8},{10,11... | collective-permute-start | bytes 11010056 | tf_op jit(solution)/shard_map/ppermute | solution.py:156
Sparse Core Ops, SparseCore 0:
  10.7 102.6 all-gather.2
  116.1 101.6 all-gather.4
  273.5 156.6 reduce-scatter.4
  433.0 159.1 reduce-scatter.2

commit v2 on v0

--- a/solution.py
+++ b/solution.py
@@ -39,7 +39,7 @@
     return (out_part, dx_part, grad_up, grad_down)
 
 
-def shards(tokens, routes, gates, upstream, w_up, w_down):
+def routed_shards(tokens, routes, gates, upstream, w_up, w_down):
     tok_rows, feature_width = tokens.shape
     top_count = routes.shape[1]
     owners = lax.axis_size("expert")
@@ -108,6 +108,143 @@
     )
 
 
+def swapped(array, bit):
+    return lax.ppermute(array, "expert", tuple((i, i ^ bit) for i in range(16)))
+
+
+def shifted(array, step, senders):
+    return lax.ppermute(array, "expert", tuple((i, i + 4 * step) for z in senders for i in range(4 * z, 4 * z + 4)))
+
+
+def add_rows(first, *others):
+    total = first.astype(jnp.float32)
+    for other in others:
+        total = total + other.astype(jnp.float32)
+    return total.astype(jnp.bfloat16)
+
+
+def gathered_slots(block, layer, first, second):
+    up_one = shifted(block, 1, (0, 1, 2))
+    down_one = shifted(block, -1, (3, 2, 1))
+    up_two = shifted(up_one, 1, (1, 2))
+    down_two = shifted(down_one, -1, (2, 1))
+    up_three = shifted(up_two, 1, (2,))
+    down_three = shifted(down_two, -1, (1,))
+    low = layer < 2
+    far = jnp.where(low, jnp.where(layer == 0, down_three, up_one), jnp.where(layer == 3, up_three, down_one))
+    columns = (block, jnp.where(low, down_one, up_one), jnp.where(low, down_two, up_two), far)
+    slots = []
+    for column in columns:
+        pair = jnp.stack([column, swapped(column, first)])
+        other = swapped(pair, second)
+        if first == 1:
+            slots.append(jnp.concatenate([pair[0], pair[1], other[0], other[1]], axis=0))
+        else:
+            slots.append(jnp.concatenate([pair[0], other[0], pair[1], other[1]], axis=0))
+    return slots
+
+
+def scattered_column(rows, tok_rows, first, second):
+    blocks = [rows[i * tok_rows : (i + 1) * tok_rows].astype(jnp.bfloat16) for i in range(4)]
+    kept, sent = ((0, 1), (2, 3)) if first == 2 else ((0, 2), (1, 3))
+    came = swapped(jnp.stack([blocks[i] for i in sent]), first)
+    near = add_rows(blocks[kept[0]], came[0])
+    far = add_rows(blocks[kept[1]], came[1])
+    return add_rows(near, swapped(far, second))
+
+
+def scattered_layers(columns, layer):
+    up = shifted(columns[3], 1, (0,))
+    down = shifted(columns[3], -1, (3,))
+    up = shifted(add_rows(columns[2], up), 1, (0, 1))
+    down = shifted(add_rows(columns[2], down), -1, (3, 2))
+    up = shifted(add_rows(jnp.where(layer == 2, columns[3], columns[1]), up), 1, (0, 1, 2))
+    down = shifted(add_rows(jnp.where(layer == 1, columns[3], columns[1]), down), -1, (3, 2, 1))
+    return add_rows(columns[0], up, down)
+
+
+def transposed_dot(rows, weights):
+    return lax.dot_general(
+        rows, weights, (((1,), (1,)), ((), ())), preferred_element_type=jnp.float32
+    )
+
+
+def outer(rows, columns):
+    return lax.dot_general(
+        rows, columns, (((0,), (0,)), ((), ())), preferred_element_type=jnp.float32
+    )
+
+
+def dense_shards(tokens, routes, gates, upstream, w_up, w_down):
+    tok_rows, width = tokens.shape
+    owners = lax.axis_size("expert")
+    half = w_up.shape[2]
+    swap = ((0, 1), (1, 0))
+    mine = lax.axis_index("expert")
+    layer = mine // 4
+    up_local, down_local = w_up[0], w_down[0]
+    named = routes[:, :, None] == jnp.arange(owners, dtype=jnp.int32)
+    gate_of = jnp.sum(jnp.where(named, gates[:, :, None], 0.0), axis=1)
+    gate_all = lax.all_gather(gate_of, "expert", axis=0, tiled=True).reshape(owners, tok_rows, owners)
+    gate_mine = lax.dynamic_index_in_dim(gate_all, mine, axis=2, keepdims=False)
+    layers = (
+        layer,
+        jnp.where(layer < 2, layer + 1, layer - 1),
+        jnp.where(layer < 2, layer + 2, layer - 2),
+        jnp.where(layer % 2 == 0, 3, 0),
+    )
+    sources = [jnp.stack([z * 4 + (mine % 4 ^ flip) for flip in range(4)]) for z in layers]
+    slots_x = gathered_slots(tokens, layer, 1, 2)
+    slots_u = gathered_slots(upstream, layer, 2, 1)
+    up_full = jnp.concatenate([up_local, lax.ppermute(up_local, "tok", swap)], axis=1)
+    down_full = jnp.concatenate([down_local, lax.ppermute(down_local, "tok", swap)], axis=0)
+    gated, slopes, inners = [None] * 4, [None] * 4, [None] * 4
+    mixed_columns, dx_columns = [None] * 4, [None] * 4
+    for s in range(4):
+        gate = gate_mine[sources[s]].reshape(-1)[:, None]
+        hidden = jnp.dot(slots_x[s], up_full, preferred_element_type=jnp.float32)
+        value = gelu_value(hidden)
+        gated[s] = (gate * value).astype(jnp.bfloat16)
+        back = transposed_dot(slots_u[s], down_full)
+        inners[s] = jnp.sum(value * back, axis=1).reshape(4, tok_rows)
+        slopes[s] = (gate * back * gelu_slope(hidden)).astype(jnp.bfloat16)
+    for s in (3, 2, 1, 0):
+        out_part = jnp.dot(gated[s], down_full, preferred_element_type=jnp.float32)
+        mixed_columns[s] = scattered_column(out_part, tok_rows, 2, 1)
+        dx_part = transposed_dot(slopes[s], up_full)
+        dx_columns[s] = scattered_column(dx_part, tok_rows, 1, 2)
+    mixed = scattered_layers(mixed_columns, layer)
+    d_tokens = scattered_layers(dx_columns, layer)
+
+    order = jnp.concatenate(sources)
+    inner = jnp.zeros((owners, tok_rows), jnp.float32).at[order].set(jnp.concatenate(inners))
+    inner_all = lax.all_gather(inner, "expert", axis=0, tiled=True).reshape(owners, owners, tok_rows)
+    home = lax.dynamic_index_in_dim(inner_all, mine, axis=1, keepdims=False)
+    d_gates = jnp.sum(jnp.where(named, home.T[:, None, :], 0.0), axis=2)
+
+    all_x, all_u = jnp.concatenate(slots_x), jnp.concatenate(slots_u)
+    act, d_hidden = jnp.concatenate(gated), jnp.concatenate(slopes)
+    down_far = outer(act[:, half:], all_u).astype(jnp.bfloat16)
+    up_far = outer(all_x, d_hidden[:, half:]).astype(jnp.bfloat16)
+    down_near = outer(act[:, :half], all_u)
+    up_near = outer(all_x, d_hidden[:, :half])
+    grad_down = down_near + lax.ppermute(down_far, "tok", swap).astype(jnp.float32)
+    grad_up = up_near + lax.ppermute(up_far, "tok", swap).astype(jnp.float32)
+    return (
+        mixed,
+        d_tokens,
+        d_gates,
+        grad_up.astype(jnp.bfloat16)[None],
+        grad_down.astype(jnp.bfloat16)[None],
+    )
+
+
+def shards(tokens, routes, gates, upstream, w_up, w_down):
+    dense = lax.axis_size("expert") == 16 and lax.axis_size("tok") == 2
+    body = dense_shards if dense else routed_shards
+    return body(tokens, routes, gates, upstream, w_up, w_down)
+
+
 def solution(mesh):
     return jax.shard_map(
         shards,

time: 625 us -> 548 us (0.88)
  local copies, waits for them, and re-layouts: 127 us -> 32.1 us
  starting transfers between devices: 20.2 us -> 109 us
  waiting for transfers between devices: 254 us -> 200 us
  blocking collectives: 105 us -> 62.5 us
  matrix products: 62 us -> 101 us
  between operations: 14.2 us -> 2 us
    all_to_all x3 -> x0, waiting for transfers between devices: 224 us -> none  [the longest x1 86.8 us: shards(): lax.all_to_all(send_x, 'expert', split_axis=0, concat_axis=0, tiled=True)]
    ppermute x0 -> x60, waiting for transfers between devices: none -> 200 us  [the longest x32 171 us: swapped(): lax.ppermute(array, 'expert', tuple(((i, i ^ bit) for i in range(16))))]
    ppermute x0 -> x60, starting transfers between devices: none -> 109 us  [the longest x24 73.5 us: shifted(): lax.ppermute(array, 'expert', tuple(((i, i + 4 * step) for z in senders f...]
    all_to_all x1 -> x0, blocking collectives: 105 us -> none  [shards(): lax.all_to_all(send_grad, 'expert', split_axis=0, concat_axis=0, tiled=True)]
    all_gather x0 -> x2, blocking collectives: none -> 62.5 us  [the longest x1 33.8 us: dense_shards(): lax.all_gather(gate_of, 'expert', axis=0, tiled=True)]
    gather x7 -> x4, local copies, waits for them, and re-layouts: 42.2 us -> 2.23 us  [dense_shards(): gate = gate_mine[sources[s]].reshape(-1)[:, None]]
    reshape x6 -> x4, local copies, waits for them, and re-layouts: 39.4 us -> 0.33 us  [dense_shards(): inners[s] = jnp.sum(value * back, axis=1).reshape(4, tok_rows)]
    dot_general x6 -> x20, matrix products: 62 us -> 101 us  [the longest x8 36.7 us: transposed_dot(): lax.dot_general(rows, weights, (((1,), (1,)), ((), ())), preferred_elemen...]
  transfers between devices with their start and end apart: 7 -> 60, of which waited for: 5 -> 28; matrix products, arithmetic and copies ran while one was open for 20% -> 25% of each run, Pallas kernels for 0% -> 0%
where the time goes in v2:
time: 548 us; the launch traced here: 542 us
  waiting for transfers between devices  200 us (36%)
  starting transfers between devices  109 us (20%)
  matrix products  101 us (18%)
  blocking collectives  62.5 us (11%)
  other arithmetic  35.2 us (6%)
  local copies, waits for them, and re-layouts  32.1 us (6%)
    ppermute x32, waiting for transfers between devices, swapped(): lax.ppermute(array, 'expert', tuple(((i, i ^ bit) for i in range(16))))  171 us
    ppermute x24, starting transfers between devices, shifted(): lax.ppermute(array, 'expert', tuple(((i, i + 4 * step) for z in senders f...  73.5 us
    dot_general x8, matrix products, transposed_dot(): lax.dot_general(rows, weights, (((1,), (1,)), ((), ())), preferred_elemen...  36.7 us
    dot_general x4, matrix products, outer(): lax.dot_general(rows, columns, (((0,), (0,)), ((), ())), preferred_elemen...  34.7 us
    ppermute x32, starting transfers between devices, swapped(): lax.ppermute(array, 'expert', tuple(((i, i ^ bit) for i in range(16))))  34.5 us
    all_gather x1, blocking collectives, dense_shards(): lax.all_gather(gate_of, 'expert', axis=0, tiled=True)  33.8 us
    ppermute x24, waiting for transfers between devices, shifted(): lax.ppermute(array, 'expert', tuple(((i, i + 4 * step) for z in senders f...  28.8 us
    all_gather x1, blocking collectives, dense_shards(): lax.all_gather(inner, 'expert', axis=0, tiled=True)  28.7 us
  transfers between devices with their start and end apart: 60, of which 28 were waited for; matrix products, arithmetic and copies ran while one was open for 25% of the time, Pallas kernels for 0%

profile of v2, /device:TPU:14, one launch (start us, length us, event | category | flops | bytes accessed | tf_op | source)
XLA Modules:
  0.0 541.7 jit_solution(3025906620837556485)
XLA Ops:
  17.9 5.5 %collective-permute-done.30 = bf16[64,3584]{1,0:T(8,128)(2,1)S(1)} collective-permute-done((bf16[64,3584]{1,0:T(8,128)(2,1)}, bf16[64,3584]{1,0:T(8,128)(2,1)S(1)}, u32[]{:S(2)}, u32[]{:S(2)}) %collective-permute-start.30) | collective-permute-done | bytes 458784 | tf_op jit(solution)/shard_map/ppermute | solution.py:112
  26.9 13.8 %collective-permute-done.1 = bf16[2,64,3584]{2,1,0:T(8,128)(2,1)S(1)} collective-permute-done((bf16[2,64,3584]{2,1,0:T(8,128)(2,1)S(1)}, bf16[2,64,3584]{2,1,0:T(8,128)(2,1)S(1)}, u32[]{:S(2)}, u32[]{:S(2)}) %collective-permute-start.1) | collective-permute-done | bytes 917536 | tf_op jit(solution)/shard_map/ppermute | solution.py:112
  43.8 16.9 %collective-permute-done.31 = bf16[2,64,3584]{2,1,0:T(8,128)(2,1)S(1)} collective-permute-done((bf16[2,64,3584]{2,1,0:T(8,128)(2,1)S(1)}, bf16[2,64,3584]{2,1,0:T(8,128)(2,1)S(1)}, u32[]{:S(2)}, u32[]{:S(2)}) %collective-permute-start.31) | collective-permute-done | bytes 917536 | tf_op jit(solution)/shard_map/ppermute | solution.py:112
  69.7 9.4 %collective-permute-done.16 = bf16[64,3584]{1,0:T(8,128)(2,1)S(1)} collective-permute-done((bf16[64,3584]{1,0:T(8,128)(2,1)S(1)}, bf16[64,3584]{1,0:T(8,128)(2,1)S(1)}, u32[]{:S(2)}, u32[]{:S(2)}) %collective-permute-start.16) | collective-permute-done | bytes 458784 | tf_op jit(solution)/shard_map/ppermute | solution.py:112
  81.3 5.5 %collective-permute-start.10 = (bf16[64,3584]{1,0:T(8,128)(2,1)S(1)}, bf16[64,3584]{1,0:T(8,128)(2,1)}, u32[]{:S(2)}, u32[]{:S(2)}) collective-permute-start(bf16[64,3584]{1,0:T(8,128)(2,1)S(1)} %copy-done.15), channel_id=1, source_target_pairs={{8,16},{10,18},{12,20},{14,22},{16,24},{18,26},{20,28},{22,30},{9,... | collective-permute-start | bytes 1376264 | tf_op jit(solution)/shard_map/ppermute | solution.py:116
  87.0 13.9 %collective-permute-done.17 = bf16[2,64,3584]{2,1,0:T(8,128)(2,1)S(1)} collective-permute-done((bf16[2,64,3584]{2,1,0:T(8,128)(2,1)S(1)}, bf16[2,64,3584]{2,1,0:T(8,128)(2,1)S(1)}, u32[]{:S(2)}, u32[]{:S(2)}) %collective-permute-start.17) | collective-permute-done | bytes 917536 | tf_op jit(solution)/shard_map/ppermute | solution.py:112
  103.8 17.8 %collective-permute-done.45 = bf16[2,64,3584]{2,1,0:T(8,128)(2,1)S(1)} collective-permute-done((bf16[2,64,3584]{2,1,0:T(8,128)(2,1)S(1)}, bf16[2,64,3584]{2,1,0:T(8,128)(2,1)S(1)}, u32[]{:S(2)}, u32[]{:S(2)}) %collective-permute-start.45) | collective-permute-done | bytes 917536 | tf_op jit(solution)/shard_map/ppermute | solution.py:112
  125.2 5.4 %collective-permute-start.38 = (bf16[64,3584]{1,0:T(8,128)(2,1)S(1)}, bf16[64,3584]{1,0:T(8,128)(2,1)}, u32[]{:S(2)}, u32[]{:S(2)}) collective-permute-start(bf16[64,3584]{1,0:T(8,128)(2,1)S(1)} %collective-permute-done.37), channel_id=1, source_target_pairs={{8,16},{10,18},{12,20},{14,22},{16,24},{18,26},{20,28},{22,30},{9,... | collective-permute-start | bytes 1376264 | tf_op jit(solution)/shard_map/ppermute | solution.py:116
  141.0 5.5 %collective-permute-done.20 = bf16[64,3584]{1,0:T(8,128)(2,1)S(1)} collective-permute-done((bf16[64,3584]{1,0:T(8,128)(2,1)S(1)}, bf16[64,3584]{1,0:T(8,128)(2,1)S(1)}, u32[]{:S(2)}, u32[]{:S(2)}) %collective-permute-start.20) | collective-permute-done | bytes 458784 | tf_op jit(solution)/shard_map/ppermute | solution.py:112
  148.6 6.4 %collective-permute-done.48 = bf16[64,3584]{1,0:T(8,128)(2,1)S(1)} collective-permute-done((bf16[64,3584]{1,0:T(8,128)(2,1)S(1)}, bf16[64,3584]{1,0:T(8,128)(2,1)S(1)}, u32[]{:S(2)}, u32[]{:S(2)}) %collective-permute-start.48) | collective-permute-done | bytes 458784 | tf_op jit(solution)/shard_map/ppermute | solution.py:112
  168.9 6.8 %multiply_reduce_fusion.2 = (f32[256]{0:T(256)S(1)}, f32[256,1024]{1,0:T(8,128)}) fusion(f32[256,1024]{1,0:T(8,128)} %fusion.18, bf16[512,3584]{1,0:T(8,128)(2,1)} %copy-done.39, bf16[512,3584]{1,0:T(8,128)(2,1)} %bitcast.290, bf16[64,3584]{1,0:T(8,128)(2,1)} %get-tuple-element.58, bf16[64,3584]{1,0:T(8,128)(2,1)S(1)} %collective-permute-done.44, ...), kind=kOutput, calls=%fused_computation.133 | convolution fusion | flops 1903689472 | bytes 11273216 | tf_op jit(solution)/shard_map/dot_general | solution.py:167
  185.7 15.2 %collective-permute-done.49 = bf16[2,64,3584]{2,1,0:T(8,128)(2,1)S(1)} collective-permute-done((bf16[2,64,3584]{2,1,0:T(8,128)(2,1)}, bf16[2,64,3584]{2,1,0:T(8,128)(2,1)S(1)}, u32[]{:S(2)}, u32[]{:S(2)}) %collective-permute-start.49) | collective-permute-done | bytes 917536 | tf_op jit(solution)/shard_map/ppermute | solution.py:112
  214.3 6.9 %collective-permute-done.40 = bf16[64,3584]{1,0:T(8,128)(2,1)S(1)} collective-permute-done((bf16[64,3584]{1,0:T(8,128)(2,1)S(1)}, bf16[64,3584]{1,0:T(8,128)(2,1)S(1)}, u32[]{:S(2)}, u32[]{:S(2)}) %collective-permute-start.40) | collective-permute-done | bytes 458784 | tf_op jit(solution)/shard_map/ppermute | solution.py:112
  223.5 7.5 %collective-permute-done.13 = bf16[2,64,3584]{2,1,0:T(8,128)(2,1)S(1)} collective-permute-done((bf16[2,64,3584]{2,1,0:T(8,128)(2,1)S(1)}, bf16[2,64,3584]{2,1,0:T(8,128)(2,1)S(1)}, u32[]{:S(2)}, u32[]{:S(2)}) %collective-permute-start.13) | collective-permute-done | bytes 917536 | tf_op jit(solution)/shard_map/ppermute | solution.py:112
  242.8 28.7 %all_gather.7 = f32[256,64]{1,0:T(8,128)S(1)} all-gather(f32[16,64]{1,0:T(8,128)S(1)} %scatter_custom_fusion), channel_id=1, replica_groups=mesh['expert'=16,'tok'=2] {'expert'}, dimensions={0}, use_global_device_ids=true | all-gather | bytes 69632 | tf_op jit(solution)/shard_map/all_gather | solution.py:221
  272.1 33.8 %all-gather = f32[16,64,16]{1,2,0:T(8,128)S(1)} all-gather(f32[1,64,16]{1,2,0:T(8,128)S(1)} %bitcast.279), channel_id=1, replica_groups=mesh['expert'=16,'tok'=2] {'expert'}, dimensions={0}, use_global_device_ids=true | all-gather | bytes 69632 | tf_op jit(solution)/shard_map/all_gather | solution.py:188
  310.9 5.3 convolution_convert_fusion.5
  326.6 5.3 convolution_convert_fusion.4
  331.9 5.3 convolution_convert_fusion.2
  352.8 5.2 convolution_convert_fusion.8
  358.1 5.2 convolution_convert_fusion.6
  366.3 8.6 %convolution_convert_fusion = bf16[512,3584]{1,0:T(8,128)(2,1)} fusion(bf16[1024,3584]{1,0:T(8,128)(2,1)} %constant_dynamic-update-slice_fusion.16, bf16[1024,1024]{1,0:T(8,128)(2,1)S(1)} %pad_maximum_fusion.3), kind=kOutput, calls=%fused_computation.9 | convolution fusion | flops 3759931392 | bytes 12058624 | tf_op jit(solution)/shard_map/dot_general | solution.py:173
  376.4 8.6 %convolution_convert_fusion.1 = bf16[3584,512]{1,0:T(8,128)(2,1)} fusion(bf16[1024,3584]{1,0:T(8,128)(2,1)} %constant_dynamic-update-slice_fusion, bf16[1024,1024]{1,0:T(8,128)(2,1)S(1)} %pad_maximum_fusion.2), kind=kOutput, calls=%fused_computation.10 | convolution fusion | flops 3759931392 | bytes 12058624 | tf_op jit(solution)/shard_map/dot_general | solution.py:173
  392.7 10.0 %collective-permute-done.18 = bf16[2,64,3584]{2,1,0:T(8,128)(2,1)S(1)} collective-permute-done((bf16[2,64,3584]{2,1,0:T(8,128)(2,1)S(1)}, bf16[2,64,3584]{2,1,0:T(8,128)(2,1)S(1)}, u32[]{:S(2)}, u32[]{:S(2)}) %collective-permute-start.18) | collective-permute-done | bytes 917536 | tf_op jit(solution)/shard_map/ppermute | solution.py:112
  405.1 23.5 %collective-permute-done.14 = bf16[2,64,3584]{2,1,0:T(8,128)(2,1)S(1)} collective-permute-done((bf16[2,64,3584]{2,1,0:T(8,128)(2,1)S(1)}, bf16[2,64,3584]{2,1,0:T(8,128)(2,1)S(1)}, u32[]{:S(2)}, u32[]{:S(2)}) %collective-permute-start.14) | collective-permute-done | bytes 917536 | tf_op jit(solution)/shard_map/ppermute | solution.py:112
  432.5 8.8 %collective-permute-done.43 = bf16[64,3584]{1,0:T(8,128)(2,1)S(1)} collective-permute-done((bf16[64,3584]{1,0:T(8,128)(2,1)S(1)}, bf16[64,3584]{1,0:T(8,128)(2,1)S(1)}, u32[]{:S(2)}, u32[]{:S(2)}) %collective-permute-start.43) | collective-permute-done | bytes 458784 | tf_op jit(solution)/shard_map/ppermute | solution.py:112
  447.1 14.2 %collective-permute-done.52 = bf16[64,3584]{1,0:T(8,128)(2,1)S(1)} collective-permute-done((bf16[64,3584]{1,0:T(8,128)(2,1)S(1)}, bf16[64,3584]{1,0:T(8,128)(2,1)S(1)}, u32[]{:S(2)}, u32[]{:S(2)}) %collective-permute-start.52) | collective-permute-done | bytes 458784 | tf_op jit(solution)/shard_map/ppermute | solution.py:116
  464.5 15.8 %collective-permute-start.53 = (bf16[64,3584]{1,0:T(8,128)(2,1)S(1)}, bf16[64,3584]{1,0:T(8,128)(2,1)S(1)}, u32[]{:S(2)}, u32[]{:S(2)}) collective-permute-start(bf16[64,3584]{1,0:T(8,128)(2,1)S(1)} %get-tuple-element.23), channel_id=1, source_target_pairs={{0,8},{2,10},{4,12},{6,14},{8,16},{10,18},{12,20},{14,22},{1,9},{3... | collective-permute-start | bytes 1376264 | tf_op jit(solution)/shard_map/ppermute | solution.py:116
  486.3 4.4 collective-permute-start.25
  517.4 4.5 collective-permute-done.29
  523.9 8.9 %fusion = bf16[1,3584,512]{2,1,0:T(8,128)(2,1)} fusion(bf16[3584,512]{1,0:T(8,128)(2,1)S(1)} %collective-permute-done.58, bf16[1024,3584]{1,0:T(8,128)(2,1)} %constant_dynamic-update-slice_fusion, bf16[1024,1024]{1,0:T(8,128)(2,1)S(1)} %pad_maximum_fusion.2), kind=kOutput, calls=%fused_computation.11 | convolution fusion | flops 3763601408 | bytes 15728640 | tf_op jit(solution)/shard_map/dot_general | solution.py:173
  532.8 8.7 %fusion.1 = bf16[1,512,3584]{2,1,0:T(8,128)(2,1)} fusion(bf16[512,3584]{1,0:T(8,128)(2,1)S(1)} %collective-permute-done.59, bf16[1024,3584]{1,0:T(8,128)(2,1)} %constant_dynamic-update-slice_fusion.16, bf16[1024,1024]{1,0:T(8,128)(2,1)S(1)} %pad_maximum_fusion.3), kind=kOutput, calls=%fused_computation.12 | convolution fusion | flops 3763601408 | bytes 15728640 | tf_op jit(solution)/shard_map/dot_general | solution.py:173
  (312 shorter events, 198.5 us)
Async XLA Ops:
  0.6 61.7 %collective-permute-start.6 = (bf16[64,3584]{1,0:T(8,128)(2,1)}, bf16[64,3584]{1,0:T(8,128)(2,1)S(1)}, u32[]{:S(2)}, u32[]{:S(2)}) collective-permute-start(bf16[64,3584]{1,0:T(8,128)(2,1)} %param.6), channel_id=1, source_target_pairs={{24,16},{26,18},{28,20},{30,22},{16,8},{18,10},{20,12},{22,14},{8,... | collective-permute-start | bytes 1376264 | tf_op jit(solution)/shard_map/ppermute | solution.py:116
  3.7 59.2 %collective-permute-start.9 = (bf16[64,3584]{1,0:T(8,128)(2,1)}, bf16[64,3584]{1,0:T(8,128)(2,1)S(1)}, u32[]{:S(2)}, u32[]{:S(2)}) collective-permute-start(bf16[64,3584]{1,0:T(8,128)(2,1)} %param.6), channel_id=1, source_target_pairs={{0,8},{2,10},{4,12},{6,14},{8,16},{10,18},{12,20},{14,22},{16,24},... | collective-permute-start | bytes 1376264 | tf_op jit(solution)/shard_map/ppermute | solution.py:116
  7.2 59.4 %collective-permute-start.34 = (bf16[64,3584]{1,0:T(8,128)(2,1)}, bf16[64,3584]{1,0:T(8,128)(2,1)S(1)}, u32[]{:S(2)}, u32[]{:S(2)}) collective-permute-start(bf16[64,3584]{1,0:T(8,128)(2,1)} %param.9), channel_id=1, source_target_pairs={{24,16},{26,18},{28,20},{30,22},{16,8},{18,10},{20,12},{22,14},{8,... | collective-permute-start | bytes 1376264 | tf_op jit(solution)/shard_map/ppermute | solution.py:116
  16.5 24.2 %collective-permute-start.1 = (bf16[2,64,3584]{2,1,0:T(8,128)(2,1)S(1)}, bf16[2,64,3584]{2,1,0:T(8,128)(2,1)S(1)}, u32[]{:S(2)}, u32[]{:S(2)}) collective-permute-start(bf16[2,64,3584]{2,1,0:T(8,128)(2,1)S(1)} %pad_maximum_fusion.4), channel_id=1, source_target_pairs={{0,4},{2,6},{4,0},{6,2},{8,12},{10,14},{12,8},{14,10},{16,20},{18,... | collective-permute-start | bytes 2752520 | tf_op jit(solution)/shard_map/ppermute | solution.py:112
  23.4 44.7 %collective-permute-start.37 = (bf16[64,3584]{1,0:T(8,128)(2,1)S(1)}, bf16[64,3584]{1,0:T(8,128)(2,1)S(1)}, u32[]{:S(2)}, u32[]{:S(2)}) collective-permute-start(bf16[64,3584]{1,0:T(8,128)(2,1)S(1)} %copy-done.1), channel_id=1, source_target_pairs={{0,8},{2,10},{4,12},{6,14},{8,16},{10,18},{12,20},{14,22},{16,24},... | collective-permute-start | bytes 1376264 | tf_op jit(solution)/shard_map/ppermute | solution.py:116
  40.7 20.0 %collective-permute-start.31 = (bf16[2,64,3584]{2,1,0:T(8,128)(2,1)S(1)}, bf16[2,64,3584]{2,1,0:T(8,128)(2,1)S(1)}, u32[]{:S(2)}, u32[]{:S(2)}) collective-permute-start(bf16[2,64,3584]{2,1,0:T(8,128)(2,1)S(1)} %pad_maximum_fusion.12), channel_id=1, source_target_pairs={{0,2},{2,0},{4,6},{6,4},{8,10},{10,8},{12,14},{14,12},{16,18},{18,... | collective-permute-start | bytes 2752520 | tf_op jit(solution)/shard_map/ppermute | solution.py:112
  60.7 97.3 %collective-permute-start.2 = (bf16[3584,512]{1,0:T(8,128)(2,1)S(1)}, bf16[3584,512]{1,0:T(8,128)(2,1)S(1)}, u32[]{:S(2)}, u32[]{:S(2)}) collective-permute-start(bf16[3584,512]{1,0:T(8,128)(2,1)S(1)} %bitcast.284), channel_id=1, source_target_pairs={{0,1},{1,0},{2,3},{3,2},{4,5},{5,4},{6,7},{7,6},{8,9},{9,8},{10,11... | collective-permute-start | bytes 11010056 | tf_op jit(solution)/shard_map/ppermute | solution.py:199
  62.4 99.9 %collective-permute-start.3 = (bf16[512,3584]{1,0:T(8,128)(2,1)S(1)}, bf16[512,3584]{1,0:T(8,128)(2,1)S(1)}, u32[]{:S(2)}, u32[]{:S(2)}) collective-permute-start(bf16[512,3584]{1,0:T(8,128)(2,1)S(1)} %bitcast.293), channel_id=1, source_target_pairs={{0,1},{1,0},{2,3},{3,2},{4,5},{5,4},{6,7},{7,6},{8,9},{9,8},{10,11... | collective-permute-start | bytes 11010056 | tf_op jit(solution)/shard_map/ppermute | solution.py:200
  62.9 62.2 %collective-permute-start.7 = (bf16[64,3584]{1,0:T(8,128)(2,1)S(1)}, bf16[64,3584]{1,0:T(8,128)(2,1)}, u32[]{:S(2)}, u32[]{:S(2)}) collective-permute-start(bf16[64,3584]{1,0:T(8,128)(2,1)S(1)} %collective-permute-done.6), channel_id=1, source_target_pairs={{16,8},{18,10},{20,12},{22,14},{8,0},{10,2},{12,4},{14,6},{17,9},{... | collective-permute-start | bytes 1376264 | tf_op jit(solution)/shard_map/ppermute | solution.py:116
  79.1 21.7 %collective-permute-start.17 = (bf16[2,64,3584]{2,1,0:T(8,128)(2,1)S(1)}, bf16[2,64,3584]{2,1,0:T(8,128)(2,1)S(1)}, u32[]{:S(2)}, u32[]{:S(2)}) collective-permute-start(bf16[2,64,3584]{2,1,0:T(8,128)(2,1)S(1)} %pad_maximum_fusion.8), channel_id=1, source_target_pairs={{0,4},{2,6},{4,0},{6,2},{8,12},{10,14},{12,8},{14,10},{16,20},{18,... | collective-permute-start | bytes 2752520 | tf_op jit(solution)/shard_map/ppermute | solution.py:112
  81.3 49.3 %collective-permute-start.10 = (bf16[64,3584]{1,0:T(8,128)(2,1)S(1)}, bf16[64,3584]{1,0:T(8,128)(2,1)}, u32[]{:S(2)}, u32[]{:S(2)}) collective-permute-start(bf16[64,3584]{1,0:T(8,128)(2,1)S(1)} %copy-done.15), channel_id=1, source_target_pairs={{8,16},{10,18},{12,20},{14,22},{16,24},{18,26},{20,28},{22,30},{9,... | collective-permute-start | bytes 1376264 | tf_op jit(solution)/shard_map/ppermute | solution.py:116
  100.9 20.7 %collective-permute-start.45 = (bf16[2,64,3584]{2,1,0:T(8,128)(2,1)S(1)}, bf16[2,64,3584]{2,1,0:T(8,128)(2,1)S(1)}, u32[]{:S(2)}, u32[]{:S(2)}) collective-permute-start(bf16[2,64,3584]{2,1,0:T(8,128)(2,1)S(1)} %pad_maximum_fusion.16), channel_id=1, source_target_pairs={{0,2},{2,0},{4,6},{6,4},{8,10},{10,8},{12,14},{14,12},{16,18},{18,... | collective-permute-start | bytes 2752520 | tf_op jit(solution)/shard_map/ppermute | solution.py:112
  130.6 51.2 %collective-permute-start.8 = (bf16[64,3584]{1,0:T(8,128)(2,1)}, bf16[64,3584]{1,0:T(8,128)(2,1)}, u32[]{:S(2)}, u32[]{:S(2)}) collective-permute-start(bf16[64,3584]{1,0:T(8,128)(2,1)} %collective-permute-done.7), channel_id=1, source_target_pairs={{8,0},{10,2},{12,4},{14,6},{9,1},{11,3},{13,5},{15,7}} | collective-permute-start | bytes 1376264 | tf_op jit(solution)/shard_map/ppermute | solution.py:116
  135.5 46.3 %collective-permute-start.11 = (bf16[64,3584]{1,0:T(8,128)(2,1)}, bf16[64,3584]{1,0:T(8,128)(2,1)}, u32[]{:S(2)}, u32[]{:S(2)}) collective-permute-start(bf16[64,3584]{1,0:T(8,128)(2,1)} %collective-permute-done.10), channel_id=1, source_target_pairs={{16,24},{18,26},{20,28},{22,30},{17,25},{19,27},{21,29},{23,31}} | collective-permute-start | bytes 1376264 | tf_op jit(solution)/shard_map/ppermute | solution.py:116
  155.0 50.6 %collective-permute-start.36 = (bf16[64,3584]{1,0:T(8,128)(2,1)}, bf16[64,3584]{1,0:T(8,128)(2,1)}, u32[]{:S(2)}, u32[]{:S(2)}) collective-permute-start(bf16[64,3584]{1,0:T(8,128)(2,1)} %collective-permute-done.35), channel_id=1, source_target_pairs={{8,0},{10,2},{12,4},{14,6},{9,1},{11,3},{13,5},{15,7}} | collective-permute-start | bytes 1376264 | tf_op jit(solution)/shard_map/ppermute | solution.py:116
  158.1 47.5 %collective-permute-start.39 = (bf16[64,3584]{1,0:T(8,128)(2,1)}, bf16[64,3584]{1,0:T(8,128)(2,1)}, u32[]{:S(2)}, u32[]{:S(2)}) collective-permute-start(bf16[64,3584]{1,0:T(8,128)(2,1)} %collective-permute-done.38), channel_id=1, source_target_pairs={{16,24},{18,26},{20,28},{22,30},{17,25},{19,27},{21,29},{23,31}} | collective-permute-start | bytes 1376264 | tf_op jit(solution)/shard_map/ppermute | solution.py:116
  179.6 21.3 %collective-permute-start.49 = (bf16[2,64,3584]{2,1,0:T(8,128)(2,1)}, bf16[2,64,3584]{2,1,0:T(8,128)(2,1)S(1)}, u32[]{:S(2)}, u32[]{:S(2)}) collective-permute-start(bf16[2,64,3584]{2,1,0:T(8,128)(2,1)} %pad_maximum_fusion.18), channel_id=1, source_target_pairs={{0,2},{2,0},{4,6},{6,4},{8,10},{10,8},{12,14},{14,12},{16,18},{18,... | collective-permute-start | bytes 2752520 | tf_op jit(solution)/shard_map/ppermute | solution.py:112
  184.2 26.9 %collective-permute-start.12 = (bf16[64,3584]{1,0:T(8,128)(2,1)}, bf16[64,3584]{1,0:T(8,128)(2,1)S(1)}, u32[]{:S(2)}, u32[]{:S(2)}) collective-permute-start(bf16[64,3584]{1,0:T(8,128)(2,1)} %get-tuple-element.14), channel_id=1, source_target_pairs={{0,2},{2,0},{4,6},{6,4},{8,10},{10,8},{12,14},{14,12},{16,18},{18,... | collective-permute-start | bytes 1376264 | tf_op jit(solution)/shard_map/ppermute | solution.py:112
  212.5 18.5 %collective-permute-start.13 = (bf16[2,64,3584]{2,1,0:T(8,128)(2,1)S(1)}, bf16[2,64,3584]{2,1,0:T(8,128)(2,1)S(1)}, u32[]{:S(2)}, u32[]{:S(2)}) collective-permute-start(bf16[2,64,3584]{2,1,0:T(8,128)(2,1)S(1)} %pad_maximum_fusion.6), channel_id=1, source_target_pairs={{0,4},{2,6},{4,0},{6,2},{8,12},{10,14},{12,8},{14,10},{16,20},{18,... | collective-permute-start | bytes 2752520 | tf_op jit(solution)/shard_map/ppermute | solution.py:112
  316.3 68.7 %collective-permute-start.32 = (bf16[2,64,3584]{2,1,0:T(8,128)(2,1)S(1)}, bf16[2,64,3584]{2,1,0:T(8,128)(2,1)}, u32[]{:S(2)}, u32[]{:S(2)}) collective-permute-start(bf16[2,64,3584]{2,1,0:T(8,128)(2,1)S(1)} %pad_maximum_fusion.13), channel_id=1, source_target_pairs={{0,2},{2,0},{4,6},{6,4},{8,10},{10,8},{12,14},{14,12},{16,18},{18,... | collective-permute-start | bytes 2752520 | tf_op jit(solution)/shard_map/ppermute | solution.py:112
  324.2 62.1 %collective-permute-start.46 = (bf16[2,64,3584]{2,1,0:T(8,128)(2,1)}, bf16[2,64,3584]{2,1,0:T(8,128)(2,1)}, u32[]{:S(2)}, u32[]{:S(2)}) collective-permute-start(bf16[2,64,3584]{2,1,0:T(8,128)(2,1)} %pad_maximum_fusion.17), channel_id=1, source_target_pairs={{0,2},{2,0},{4,6},{6,4},{8,10},{10,8},{12,14},{14,12},{16,18},{18,... | collective-permute-start | bytes 2752520 | tf_op jit(solution)/shard_map/ppermute | solution.py:112
  337.4 52.0 %collective-permute-start.50 = (bf16[2,64,3584]{2,1,0:T(8,128)(2,1)S(1)}, bf16[2,64,3584]{2,1,0:T(8,128)(2,1)S(1)}, u32[]{:S(2)}, u32[]{:S(2)}) collective-permute-start(bf16[2,64,3584]{2,1,0:T(8,128)(2,1)S(1)} %pad_maximum_fusion.19), channel_id=1, source_target_pairs={{0,2},{2,0},{4,6},{6,4},{8,10},{10,8},{12,14},{14,12},{16,18},{18,... | collective-permute-start | bytes 2752520 | tf_op jit(solution)/shard_map/ppermute | solution.py:112
  339.1 50.7 %collective-permute-start.42 = (bf16[2,64,3584]{2,1,0:T(8,128)(2,1)S(1)}, bf16[2,64,3584]{2,1,0:T(8,128)(2,1)}, u32[]{:S(2)}, u32[]{:S(2)}) collective-permute-start(bf16[2,64,3584]{2,1,0:T(8,128)(2,1)S(1)} %pad_maximum_fusion.15), channel_id=1, source_target_pairs={{0,2},{2,0},{4,6},{6,4},{8,10},{10,8},{12,14},{14,12},{16,18},{18,... | collective-permute-start | bytes 2752520 | tf_op jit(solution)/shard_map/ppermute | solution.py:112
  344.1 46.9 %collective-permute-start.4 = (bf16[2,64,3584]{2,1,0:T(8,128)(2,1)S(1)}, bf16[2,64,3584]{2,1,0:T(8,128)(2,1)}, u32[]{:S(2)}, u32[]{:S(2)}) collective-permute-start(bf16[2,64,3584]{2,1,0:T(8,128)(2,1)S(1)} %pad_maximum_fusion.5), channel_id=1, source_target_pairs={{0,4},{2,6},{4,0},{6,2},{8,12},{10,14},{12,8},{14,10},{16,20},{18,... | collective-permute-start | bytes 2752520 | tf_op jit(solution)/shard_map/ppermute | solution.py:112
  386.3 44.4 %collective-permute-start.22 = (bf16[2,64,3584]{2,1,0:T(8,128)(2,1)S(1)}, bf16[2,64,3584]{2,1,0:T(8,128)(2,1)S(1)}, u32[]{:S(2)}, u32[]{:S(2)}) collective-permute-start(bf16[2,64,3584]{2,1,0:T(8,128)(2,1)S(1)} %pad_maximum_fusion.11), channel_id=1, source_target_pairs={{0,4},{2,6},{4,0},{6,2},{8,12},{10,14},{12,8},{14,10},{16,20},{18,... | collective-permute-start | bytes 2752520 | tf_op jit(solution)/shard_map/ppermute | solution.py:112
  389.4 39.2 %collective-permute-start.14 = (bf16[2,64,3584]{2,1,0:T(8,128)(2,1)S(1)}, bf16[2,64,3584]{2,1,0:T(8,128)(2,1)S(1)}, u32[]{:S(2)}, u32[]{:S(2)}) collective-permute-start(bf16[2,64,3584]{2,1,0:T(8,128)(2,1)S(1)} %pad_maximum_fusion.7), channel_id=1, source_target_pairs={{0,4},{2,6},{4,0},{6,2},{8,12},{10,14},{12,8},{14,10},{16,20},{18,... | collective-permute-start | bytes 2752520 | tf_op jit(solution)/shard_map/ppermute | solution.py:112
  389.8 134.1 %collective-permute-start.58 = (bf16[3584,512]{1,0:T(8,128)(2,1)S(1)}, bf16[3584,512]{1,0:T(8,128)(2,1)S(1)}, u32[]{:S(2)}, u32[]{:S(2)}) collective-permute-start(bf16[3584,512]{1,0:T(8,128)(2,1)S(1)} %copy-done.45), channel_id=1, source_target_pairs={{0,1},{1,0},{2,3},{3,2},{4,5},{5,4},{6,7},{7,6},{8,9},{9,8},{10,11... | collective-permute-start | bytes 11010056 | tf_op jit(solution)/shard_map/ppermute | solution.py:232
  391.0 141.8 %collective-permute-start.59 = (bf16[512,3584]{1,0:T(8,128)(2,1)}, bf16[512,3584]{1,0:T(8,128)(2,1)S(1)}, u32[]{:S(2)}, u32[]{:S(2)}) collective-permute-start(bf16[512,3584]{1,0:T(8,128)(2,1)} %convolution_convert_fusion), channel_id=1, source_target_pairs={{0,1},{1,0},{2,3},{3,2},{4,5},{5,4},{6,7},{7,6},{8,9},{9,8},{10,11... | collective-permute-start | bytes 11010056 | tf_op jit(solution)/shard_map/ppermute | solution.py:231
  402.7 42.0 %collective-permute-start.51 = (bf16[64,3584]{1,0:T(8,128)(2,1)S(1)}, bf16[64,3584]{1,0:T(8,128)(2,1)S(1)}, u32[]{:S(2)}, u32[]{:S(2)}) collective-permute-start(bf16[64,3584]{1,0:T(8,128)(2,1)S(1)} %fusion.102), channel_id=1, source_target_pairs={{0,4},{2,6},{4,0},{6,2},{8,12},{10,14},{12,8},{14,10},{16,20},{18,... | collective-permute-start | bytes 1376264 | tf_op jit(solution)/shard_map/ppermute | solution.py:112
  461.3 19.0 %collective-permute-start.24 = (bf16[64,3584]{1,0:T(8,128)(2,1)S(1)}, bf16[64,3584]{1,0:T(8,128)(2,1)S(1)}, u32[]{:S(2)}, u32[]{:S(2)}) collective-permute-start(bf16[64,3584]{1,0:T(8,128)(2,1)S(1)} %add_convert_fusion.14), channel_id=1, source_target_pairs={{0,8},{2,10},{4,12},{6,14},{1,9},{3,11},{5,13},{7,15}} | collective-permute-start | bytes 1376264 | tf_op jit(solution)/shard_map/ppermute | solution.py:116
  462.9 19.0 %collective-permute-start.47 = (bf16[64,3584]{1,0:T(8,128)(2,1)S(1)}, bf16[64,3584]{1,0:T(8,128)(2,1)S(1)}, u32[]{:S(2)}, u32[]{:S(2)}) collective-permute-start(bf16[64,3584]{1,0:T(8,128)(2,1)S(1)} %fusion.104), channel_id=1, source_target_pairs={{0,4},{2,6},{4,0},{6,2},{8,12},{10,14},{12,8},{14,10},{16,20},{18,... | collective-permute-start | bytes 1376264 | tf_op jit(solution)/shard_map/ppermute | solution.py:112
  464.5 21.7 %collective-permute-start.53 = (bf16[64,3584]{1,0:T(8,128)(2,1)S(1)}, bf16[64,3584]{1,0:T(8,128)(2,1)S(1)}, u32[]{:S(2)}, u32[]{:S(2)}) collective-permute-start(bf16[64,3584]{1,0:T(8,128)(2,1)S(1)} %get-tuple-element.23), channel_id=1, source_target_pairs={{0,8},{2,10},{4,12},{6,14},{8,16},{10,18},{12,20},{14,22},{1,9},{3... | collective-permute-start | bytes 1376264 | tf_op jit(solution)/shard_map/ppermute | solution.py:116
  (74 other events, 1021.1 us)
